TPU v7x, 256 devices: a whole 4x4x8 slice. The times are simulated.
256 devices in a mesh: seg: 32 (over x, z), tp: 8 (over y, core).
Axes of the slice: x: 4, y: 4, z: 8, core: 2. Of those that a mesh axis runs over, the one named last changes fastest.
Arguments:
- queries: bfloat16 [8192, 8192], P('seg', 'tp'), may hold values from -8 to 8
- keys_own: bfloat16 [8192, 1024], P('seg', 'tp'), may hold values from -8 to 8
- values_own: bfloat16 [8192, 1024], P('seg', 'tp'), may hold values from -6 to 6
- out_grad: bfloat16 [8192, 8192], P('seg', 'tp'), may hold values from -6 to 6
- summary_states: bfloat16 [1600, 8192], P('seg'), may hold values from -6 to 6
- w_key: bfloat16 [8192, 1024], P(None, 'tp'), may hold values from -0.0625 to 0.0625
- w_value: bfloat16 [8192, 1024], P(None, 'tp'), may hold values from -0.0625 to 0.0625
- summary_grad: bfloat16 [1600, 8192], P('seg', 'tp'), may hold values from -6 to 6
Outputs:
- query_grad: bfloat16 [8192, 8192], P('seg', 'tp')
- key_grad: bfloat16 [8192, 1024], P('seg', 'tp')
- value_grad: bfloat16 [8192, 1024], P('seg', 'tp')
- state_grad: bfloat16 [1600, 8192], P('seg', 'tp')
All inputs are finite; a program needn't handle non-finite values.
Results may differ from a plain program's by a relative error of at most 0.023.
Values may be sent and summed in bfloat16 or wider, within the bound.
A program may use at most 256 MiB of HBM per device.

v0:
```python
import jax
import jax.numpy as jnp
from jax import lax
from jax.sharding import PartitionSpec as P

HEADS = 64
KVH = 8
HD = 128


def per_device(
    queries, keys_own, values_own, out_grad, summary_states, w_key, w_value, summary_grad
):
    rows = queries.shape[0]
    kv_local = keys_own.shape[1] // HD
    group = HEADS // KVH
    scale = HD ** (-0.5)
    count = summary_states.shape[0]
    segments = lax.axis_size("seg")
    position = lax.axis_index("seg")
    nsum = count * segments
    nkeys = nsum + rows
    width = kv_local * HD
    projected = jnp.concatenate(
        [
            jnp.dot(summary_states, w_key, preferred_element_type=jnp.float32).astype(jnp.bfloat16),
            jnp.dot(summary_states, w_value, preferred_element_type=jnp.float32).astype(
                jnp.bfloat16
            ),
        ],
        axis=1,
    )
    everyone = lax.all_gather(projected, "seg", axis=0, tiled=True)
    keys_all = jnp.concatenate([everyone[:, :width], keys_own], 0)
    vals_all = jnp.concatenate([everyone[:, width:], values_own], 0)
    row_pos = jnp.arange(rows)[:, None]
    col_pos = jnp.arange(nkeys)[None, :]
    visible = jnp.where(col_pos < nsum, col_pos < position * count, col_pos - nsum <= row_pos)
    query_heads = queries.reshape(rows, kv_local * group, HD).transpose(1, 0, 2)
    grad_heads = out_grad.reshape(rows, kv_local * group, HD).transpose(1, 0, 2)
    contract_last = (((1,), (1,)), ((), ()))
    contract_first = (((0,), (0,)), ((), ()))

    def head_step(carry, inputs):
        key_acc, val_acc = carry
        query_head, grad_head = inputs
        scores = (
            lax.dot_general(query_head, keys_all, contract_last, preferred_element_type=jnp.float32)
            * scale
        )
        scores = jnp.where(visible, scores, -jnp.inf)
        probs = jnp.exp(scores - jnp.max(scores, axis=-1, keepdims=True))
        probs = probs / jnp.sum(probs, axis=-1, keepdims=True)
        probs_b = probs.astype(jnp.bfloat16)
        attn = jnp.dot(probs_b, vals_all, preferred_element_type=jnp.float32)
        delta = jnp.sum(grad_head.astype(jnp.float32) * attn, axis=-1)
        dprobs = lax.dot_general(
            grad_head, vals_all, contract_last, preferred_element_type=jnp.float32
        )
        dscores = (probs * (dprobs - delta[:, None])).astype(jnp.bfloat16)
        dquery = (jnp.dot(dscores, keys_all, preferred_element_type=jnp.float32) * scale).astype(
            jnp.bfloat16
        )
        key_acc = key_acc + lax.dot_general(
            dscores, query_head, contract_first, preferred_element_type=jnp.float32
        )
        val_acc = val_acc + lax.dot_general(
            probs_b, grad_head, contract_first, preferred_element_type=jnp.float32
        )
        return ((key_acc, val_acc), dquery)

    zeros = jnp.zeros((nkeys, HD), jnp.float32)
    (key_acc, val_acc), dquery = lax.scan(head_step, (zeros, zeros), (query_heads, grad_heads))
    key_sums = [key_acc * scale]
    value_sums = [val_acc]
    query_grad = dquery.transpose(1, 0, 2).reshape(rows, kv_local * group * HD)
    key_grad = jnp.concatenate([acc[nsum:] for acc in key_sums], 1).astype(jnp.bfloat16)
    value_grad = jnp.concatenate([acc[nsum:] for acc in value_sums], 1).astype(jnp.bfloat16)
    summary_terms = jnp.concatenate(
        [acc[:nsum] for acc in key_sums] + [acc[:nsum] for acc in value_sums], 1
    )
    emitted = lax.psum_scatter(
        summary_terms.astype(jnp.bfloat16), "seg", scatter_dimension=0, tiled=True
    )
    partial_state = lax.dot_general(
        emitted[:, :width], w_key, contract_last, preferred_element_type=jnp.float32
    )
    partial_state = partial_state + lax.dot_general(
        emitted[:, width:], w_value, contract_last, preferred_element_type=jnp.float32
    )
    shared = lax.psum_scatter(
        partial_state.astype(jnp.bfloat16), "tp", scatter_dimension=1, tiled=True
    ).astype(jnp.float32)
    state_grad = (shared + summary_grad.astype(jnp.float32)).astype(jnp.bfloat16)
    return (query_grad, key_grad, value_grad, state_grad)


def solution(mesh):
    placed = (
        P("seg", "tp"),
        P("seg", "tp"),
        P("seg", "tp"),
        P("seg", "tp"),
        P("seg", None),
        P(None, "tp"),
        P(None, "tp"),
        P("seg", "tp"),
    )
    return jax.shard_map(
        per_device,
        mesh=mesh,
        in_specs=placed,
        out_specs=(P("seg", "tp"), P("seg", "tp"), P("seg", "tp"), P("seg", "tp")),
        check_vma=False,
    )
```

profile of v0, /device:TPU:6, one launch (start us, length us, event | category | flops | bytes accessed | tf_op | source)
XLA Modules:
  0.0 369.8 jit_solution(2039793102110522160)
XLA Ops:
  7.3 2.5 convolution_convert_fusion
  10.4 52.5 %all-gather = bf16[32,50,256]{2,1,0:T(8,128)(2,1)S(1)} all-gather(bf16[1,50,256]{2,1,0:T(8,128)(2,1)S(1)} %maximum_bitcast_fusion), channel_id=1, replica_groups=mesh['seg'=32,'tp'=8] {'seg'}, dimensions={0}, use_global_device_ids=true | all-gather | bytes 844800 | tf_op jit(solution)/shard_map/all_gather | solution.py:33
  62.9 1.1 reshape.39
  64.0 1.2 fusion.31
  65.3 2.0 copy.18
  67.3 2.0 copy.19
  70.2 105.0 %while.15 = (s32[]{:T(128)}, f32[1856,128]{1,0:T(8,128)}, f32[1856,128]{1,0:T(8,128)}, bf16[8,256,128]{2,1,0:T(8,128)(2,1)}, bf16[8,256,128]{1,2,0:T(8,128)(2,1)...) while((s32[]{:T(128)}, f32[1856,128]{1,0:T(8,128)}, ...), condition=%wide.region_4.5_spmd.clone, body=%wide.region_0.4_spmd.clone.sunk | while | flops 738049280 | bytes 25123396 | solution.py:73
  70.2 1.7 fusion.75
  73.3 1.2 fusion.78
  74.5 2.3 fusion.79
  76.8 2.6 convolution_add_fusion.5
  79.4 1.1 fusion.80
  80.5 2.2 convolution_add_fusion.6
  82.8 1.7 fusion.75
  85.8 1.2 fusion.78
  87.0 2.3 fusion.79
  89.3 2.9 convolution_add_fusion.5
  92.3 1.1 fusion.80
  93.4 2.6 convolution_add_fusion.6
  96.0 1.7 fusion.75
  99.0 1.2 fusion.78
  100.2 2.3 fusion.79
  102.5 2.9 convolution_add_fusion.5
  105.5 1.1 fusion.80
  106.6 2.6 convolution_add_fusion.6
  109.2 1.7 fusion.75
  112.2 1.2 fusion.78
  113.4 2.3 fusion.79
  115.7 2.9 convolution_add_fusion.5
  118.7 1.1 fusion.80
  119.8 2.6 convolution_add_fusion.6
  122.4 1.7 fusion.75
  125.4 1.2 fusion.78
  126.6 2.3 fusion.79
  129.0 2.9 convolution_add_fusion.5
  131.9 1.1 fusion.80
  133.0 2.6 convolution_add_fusion.6
  135.6 1.7 fusion.75
  138.6 1.2 fusion.78
  139.8 2.3 fusion.79
  142.2 2.9 convolution_add_fusion.5
  145.1 1.1 fusion.80
  146.2 2.6 convolution_add_fusion.6
  148.8 1.7 fusion.75
  151.9 1.2 fusion.78
  153.1 2.3 fusion.79
  155.4 2.9 convolution_add_fusion.5
  158.3 1.1 fusion.80
  159.4 2.6 convolution_add_fusion.6
  162.0 1.7 fusion.75
  165.1 1.2 fusion.78
  166.3 2.3 fusion.79
  168.6 2.9 convolution_add_fusion.5
  171.5 1.1 fusion.80
  172.6 2.6 convolution_add_fusion.6
  175.2 1.3 multiply_convert_fusion
  176.5 1.2 convert.11
  177.8 1.0 pad_maximum_fusion
  180.2 143.3 %all-reduce.3.cloned.1.call-done = bf16[1600,256]{1,0:T(8,128)(2,1)} async-done(((bf16[1600,256]{1,0:T(8,128)(2,1)}), bf16[1600,256]{1,0:T(8,128)(2,1)}) %all-reduce.3.cloned.1.call-update) | async-done | bytes 819216
  323.4 2.2 fusion.27
  325.6 3.0 fusion.25
  330.0 1.9 copy_bitcast_fusion
  331.9 29.5 %reduce-scatter.2.cloned.1.call-done = bf16[50,1024]{1,0:T(8,128)(2,1)} async-done(((bf16[50,8192]{1,0:T(8,128)(2,1)}), bf16[50,1024]{1,0:T(8,128)(2,1)}) %reduce-scatter.2.cloned.1.call-update) | async-done | bytes 102416 | tf_op jit(solution)/shard_map/reduce_scatter | solution.py:91
  361.4 1.6 add_convert_fusion
  (79 shorter events, 14.4 us)
Async XLA Ops:
  7.2 2.6 copy-start
  7.2 2.7 copy-start.3
  7.2 316.2 %all-reduce.3.cloned.1.call-start = ((), (), s32[]{:S(2)}) async-start(), calls=%async_computation.2 | async-start | bytes 1638400
  64.0 5.3 %copy-start.6 = (bf16[256,128]{1,0:T(8,128)(2,1)S(1)}, bf16[256,128]{1,0:T(8,128)(2,1)}, u32[]{:S(2)}) copy-start(bf16[256,128]{1,0:T(8,128)(2,1)} %param.11) | copy-start | bytes 196612
  64.0 5.3 %copy-start.7 = (bf16[256,128]{1,0:T(8,128)(2,1)S(1)}, bf16[256,128]{1,0:T(8,128)(2,1)}, u32[]{:S(2)}) copy-start(bf16[256,128]{1,0:T(8,128)(2,1)} %param.12) | copy-start | bytes 196612
  72.2 1.0 copy-start.4
  76.8 2.6 copy-start.1
  84.8 1.0 copy-start.4
  89.3 3.0 copy-start.1
  98.0 1.0 copy-start.4
  102.5 2.9 copy-start.1
  111.2 1.0 copy-start.4
  115.7 2.9 copy-start.1
  124.4 1.0 copy-start.4
  128.9 3.0 copy-start.1
  137.6 1.0 copy-start.4
  142.2 2.9 copy-start.1
  150.8 1.0 copy-start.4
  155.4 2.9 copy-start.1
  164.0 1.0 copy-start.4
  168.6 2.9 copy-start.1
  177.8 1.1 copy-start.8
  178.8 182.5 %reduce-scatter.2.cloned.1.call-start = ((), (), s32[]{:S(2)}) async-start(), calls=%async_computation.1 | async-start | bytes 1032192 | tf_op jit(solution)/shard_map/reduce_scatter | solution.py:91
  323.4 2.2 copy-start.2
  328.7 32.7 %copy-start.5 = (bf16[50,1024]{1,0:T(8,128)(2,1)S(1)}, bf16[50,1024]{1,0:T(8,128)(2,1)}, u32[]{:S(2)}) copy-start(bf16[50,1024]{1,0:T(8,128)(2,1)} %param.17) | copy-start | bytes 307204
Sparse Core Ops, SparseCore 0:
  179.0 144.4 all-reduce.2
  328.8 32.4 reduce-scatter.1
where the time goes:
time: 372 us; the launch traced here: 370 us
  waiting for transfers between devices  173 us (47%)
  matrix products  102 us (27%)
  blocking collectives  52.5 us (14%)
  local copies, waits for them, and re-layouts  16.2 us (4%)
  between operations  14.8 us (4%)
  other arithmetic  11 us (3%)
    unnamed x3, waiting for transfers between devices  143 us
    all_gather x1, blocking collectives, per_device(): everyone = lax.all_gather(projected, 'seg', axis=0, tiled=True)  52.5 us
    reduce_scatter x1, waiting for transfers between devices, per_device(): lax.psum_scatter(partial_state.astype(jnp.bfloat16), 'tp', scatter_dimens...  29.5 us
    dot_general x8, matrix products, head_step(): lax.dot_general(dscores, query_head, contract_first, preferred_element_ty...  23.3 us
    dot_general x8, matrix products, head_step(): lax.dot_general(probs_b, grad_head, contract_first, preferred_element_typ...  20.5 us
    dot_general x8, matrix products, head_step(): lax.dot_general(grad_head, vals_all, contract_last, preferred_element_typ...  18.6 us
    dot_general x8, matrix products, head_step(): lax.dot_general(query_head, keys_all, contract_last, preferred_element_ty...  13.3 us
    dot_general x8, matrix products, head_step(): attn = jnp.dot(probs_b, vals_all, preferred_element_type=jnp.float32)  9.62 us
  transfers between devices with their start and end apart: 2, of which 2 were waited for; matrix products, arithmetic and copies ran while one was open for 1% of the time, Pallas kernels for 0%

commit v1 on v0

--- a/solution.py
+++ b/solution.py
@@ -30,7 +30,9 @@
         ],
         axis=1,
     )
-    everyone = lax.all_gather(projected, "seg", axis=0, tiled=True)
+    everyone = jnp.concatenate(
+        lax.all_to_all(jnp.stack([projected] * lax.axis_size("seg")), "seg", 0, 0), axis=0
+    )
     keys_all = jnp.concatenate([everyone[:, :width], keys_own], 0)
     vals_all = jnp.concatenate([everyone[:, width:], values_own], 0)
     row_pos = jnp.arange(rows)[:, None]

time: 372 us -> 352 us (0.946)
  blocking collectives: 52.5 us -> 0 us
  waiting for transfers between devices: 173 us -> 194 us
  starting transfers between devices: 0.08 us -> 11.7 us
    all_gather x1 -> x0, blocking collectives: 52.5 us -> none  [per_device(): everyone = lax.all_gather(projected, 'seg', axis=0, tiled=True)]
    all_to_all x0 -> x1, waiting for transfers between devices: none -> 20.6 us  [per_device(): lax.all_to_all(jnp.stack([projected] * lax.axis_size('seg')), 'seg', 0, 0)]
    all_to_all x0 -> x1, starting transfers between devices: none -> 11.6 us  [per_device(): lax.all_to_all(jnp.stack([projected] * lax.axis_size('seg')), 'seg', 0, 0)]
  transfers between devices with their start and end apart: 2 -> 3, of which waited for: 2 -> 3; matrix products, arithmetic and copies ran while one was open for 1% -> 2% of each run, Pallas kernels for 0% -> 0%
where the time goes in v1:
time: 352 us; the launch traced here: 349 us
  waiting for transfers between devices  194 us (55%)
  matrix products  102 us (29%)
  local copies, waits for them, and re-layouts  16.2 us (5%)
  between operations  14.9 us (4%)
  starting transfers between devices  11.7 us (3%)
  other arithmetic  11 us (3%)
    unnamed x3, waiting for transfers between devices  143 us
    reduce_scatter x1, waiting for transfers between devices, per_device(): lax.psum_scatter(partial_state.astype(jnp.bfloat16), 'tp', scatter_dimens...  29.4 us
    dot_general x8, matrix products, head_step(): lax.dot_general(dscores, query_head, contract_first, preferred_element_ty...  23.1 us
    all_to_all x1, waiting for transfers between devices, per_device(): lax.all_to_all(jnp.stack([projected] * lax.axis_size('seg')), 'seg', 0, 0)  20.6 us
    dot_general x8, matrix products, head_step(): lax.dot_general(probs_b, grad_head, contract_first, preferred_element_typ...  20.5 us
    dot_general x8, matrix products, head_step(): lax.dot_general(grad_head, vals_all, contract_last, preferred_element_typ...  18.4 us
    dot_general x8, matrix products, head_step(): lax.dot_general(query_head, keys_all, contract_last, preferred_element_ty...  13.3 us
    all_to_all x1, starting transfers between devices, per_device(): lax.all_to_all(jnp.stack([projected] * lax.axis_size('seg')), 'seg', 0, 0)  11.6 us
  transfers between devices with their start and end apart: 3, of which 3 were waited for; matrix products, arithmetic and copies ran while one was open for 2% of the time, Pallas kernels for 0%

profile of v1, /device:TPU:6, one launch (start us, length us, event | category | flops | bytes accessed | tf_op | source)
XLA Modules:
  0.0 349.4 jit_solution(14604607582383560026)
XLA Ops:
  7.2 2.5 convolution_convert_fusion
  10.4 1.0 stack.2
  11.4 11.6 %all-to-all-start = ((bf16[32,50,256]{2,1,0:T(8,128)(2,1)}), bf16[32,50,256]{2,1,0:T(8,128)(2,1)S(1)}, u32[]{:S(2)}, u32[]{:S(2)}) async-start(bf16[32,50,256]{2,1,0:T(8,128)(2,1)} %stack.2), calls=%async_computation | async-start | bytes 1835008 | tf_op jit(solution)/shard_map/all_to_all | solution.py:34
  24.1 2.0 copy.19
  26.2 20.6 %all-to-all-done = bf16[32,50,256]{2,1,0:T(8,128)(2,1)S(1)} async-done(((bf16[32,50,256]{2,1,0:T(8,128)(2,1)}), bf16[32,50,256]{2,1,0:T(8,128)(2,1)S(1)}, u32[]{:S(2)}, u32[]{:S(2)}) %all-to-all-start) | async-done | bytes 819232 | tf_op jit(solution)/shard_map/all_to_all | solution.py:34
  46.8 1.1 reshape.41
  48.0 1.2 fusion.31
  50.0 104.8 %while.15 = (s32[]{:T(128)}, f32[1856,128]{1,0:T(8,128)}, f32[1856,128]{1,0:T(8,128)}, bf16[8,256,128]{2,1,0:T(8,128)(2,1)}, bf16[8,256,128]{1,2,0:T(8,128)(2,1)...) while((s32[]{:T(128)}, f32[1856,128]{1,0:T(8,128)}, ...), condition=%wide.region_4.5_spmd.clone, body=%wide.region_0.4_spmd.clone.sunk | while | flops 738049280 | bytes 25123396 | solution.py:75
  50.0 1.7 fusion.75
  53.0 1.2 fusion.78
  54.2 2.3 fusion.79
  56.5 2.6 convolution_add_fusion.5
  59.2 1.1 fusion.80
  60.3 2.2 convolution_add_fusion.6
  62.5 1.7 fusion.75
  65.5 1.2 fusion.78
  66.7 2.3 fusion.79
  69.1 2.9 convolution_add_fusion.5
  72.0 1.1 fusion.80
  73.1 2.6 convolution_add_fusion.6
  75.7 1.7 fusion.75
  78.7 1.2 fusion.78
  79.9 2.3 fusion.79
  82.2 2.9 convolution_add_fusion.5
  85.2 1.1 fusion.80
  86.3 2.6 convolution_add_fusion.6
  88.9 1.7 fusion.75
  91.9 1.2 fusion.78
  93.1 2.3 fusion.79
  95.4 2.9 convolution_add_fusion.5
  98.3 1.1 fusion.80
  99.4 2.6 convolution_add_fusion.6
  102.1 1.7 fusion.75
  105.1 1.2 fusion.78
  106.3 2.3 fusion.79
  108.6 2.9 convolution_add_fusion.5
  111.5 1.1 fusion.80
  112.6 2.6 convolution_add_fusion.6
  115.2 1.7 fusion.75
  118.3 1.2 fusion.78
  119.5 2.3 fusion.79
  121.8 2.9 convolution_add_fusion.5
  124.7 1.1 fusion.80
  125.8 2.6 convolution_add_fusion.6
  128.4 1.7 fusion.75
  131.5 1.2 fusion.78
  132.7 2.3 fusion.79
  135.0 2.9 convolution_add_fusion.5
  137.9 1.1 fusion.80
  139.0 2.6 convolution_add_fusion.6
  141.6 1.7 fusion.75
  144.7 1.2 fusion.78
  145.9 2.3 fusion.79
  148.2 2.9 convolution_add_fusion.5
  151.1 1.1 fusion.80
  152.2 2.6 convolution_add_fusion.6
  154.8 1.3 multiply_convert_fusion
  156.1 1.2 convert.11
  159.7 143.4 %all-reduce.3.cloned.1.call-done = bf16[1600,256]{1,0:T(8,128)(2,1)} async-done(((bf16[1600,256]{1,0:T(8,128)(2,1)}), bf16[1600,256]{1,0:T(8,128)(2,1)}) %all-reduce.3.cloned.1.call-update) | async-done | bytes 819216
  303.1 2.2 fusion.27
  305.3 3.0 fusion.25
  309.7 1.9 copy_bitcast_fusion
  311.6 29.4 %reduce-scatter.2.cloned.1.call-done = bf16[50,1024]{1,0:T(8,128)(2,1)} async-done(((bf16[50,8192]{1,0:T(8,128)(2,1)}), bf16[50,1024]{1,0:T(8,128)(2,1)}) %reduce-scatter.2.cloned.1.call-update) | async-done | bytes 102416 | tf_op jit(solution)/shard_map/reduce_scatter | solution.py:93
  341.0 1.6 add_convert_fusion
  (83 shorter events, 16.5 us)
Async XLA Ops:
  7.2 2.5 copy-start
  7.2 2.7 copy-start.3
  10.4 12.7 %copy-start.4 = (bf16[256,1024]{1,0:T(8,128)(2,1)S(1)}, bf16[256,1024]{1,0:T(8,128)(2,1)}, u32[]{:S(2)}) copy-start(bf16[256,1024]{1,0:T(8,128)(2,1)} %param.10) | copy-start | bytes 1572868
  11.4 35.4 %all-to-all-start = ((bf16[32,50,256]{2,1,0:T(8,128)(2,1)}), bf16[32,50,256]{2,1,0:T(8,128)(2,1)S(1)}, u32[]{:S(2)}, u32[]{:S(2)}) async-start(bf16[32,50,256]{2,1,0:T(8,128)(2,1)} %stack.2), calls=%async_computation | async-start | bytes 1835008 | tf_op jit(solution)/shard_map/all_to_all | solution.py:34
  23.0 280.1 %all-reduce.3.cloned.1.call-start = ((), (), s32[]{:S(2)}) async-start(), calls=%async_computation.3 | async-start | bytes 1638400
  26.2 23.0 %copy-start.7 = (bf16[256,128]{1,0:T(8,128)(2,1)S(1)}, bf16[256,128]{1,0:T(8,128)(2,1)}, u32[]{:S(2)}) copy-start(bf16[256,128]{1,0:T(8,128)(2,1)} %param.11) | copy-start | bytes 196612
  26.2 23.0 %copy-start.8 = (bf16[256,128]{1,0:T(8,128)(2,1)S(1)}, bf16[256,128]{1,0:T(8,128)(2,1)}, u32[]{:S(2)}) copy-start(bf16[256,128]{1,0:T(8,128)(2,1)} %param.12) | copy-start | bytes 196612
  52.0 1.0 copy-start.5
  56.5 2.6 copy-start.1
  64.5 1.0 copy-start.5
  69.1 2.9 copy-start.1
  77.7 1.0 copy-start.5
  82.2 2.9 copy-start.1
  90.9 1.0 copy-start.5
  95.4 2.9 copy-start.1
  104.0 1.0 copy-start.5
  108.6 2.9 copy-start.1
  117.2 1.0 copy-start.5
  121.8 2.9 copy-start.1
  130.4 1.0 copy-start.5
  135.0 2.9 copy-start.1
  143.6 1.0 copy-start.5
  148.2 2.9 copy-start.1
  157.4 1.1 copy-start.9
  158.4 182.6 %reduce-scatter.2.cloned.1.call-start = ((), (), s32[]{:S(2)}) async-start(), calls=%async_computation.2 | async-start | bytes 1032192 | tf_op jit(solution)/shard_map/reduce_scatter | solution.py:93
  303.1 2.2 copy-start.2
  308.4 32.6 %copy-start.6 = (bf16[50,1024]{1,0:T(8,128)(2,1)S(1)}, bf16[50,1024]{1,0:T(8,128)(2,1)}, u32[]{:S(2)}) copy-start(bf16[50,1024]{1,0:T(8,128)(2,1)} %param.17) | copy-start | bytes 307204
Sparse Core Ops, SparseCore 0:
  158.5 144.5 all-reduce.2
  308.5 32.4 reduce-scatter.1
